TPU v7x, 128 devices: a whole 4x4x4 slice. The times are simulated.
128 devices in a mesh: grp: 8 (over z, core), sub: 16 (over x, y).
Axes of the slice: x: 4, y: 4, z: 4, core: 2. Of those that a mesh axis runs over, the one named last changes fastest.
Arguments:
- rhs: float32 [96, 131072], P(None, ('grp', 'sub')), may hold values from -13 to 13
- blocks: bfloat16 [16384, 6656], P(('grp', 'sub')), may hold values from -0.05 to 0.45, as said below
- owners: int32 [16384, 1], P(('grp', 'sub')), may hold values from 0 to 7; in each aligned block of 128 rows (0 to 127, 128 to 255, ...) at most 48 rows name the same one
- conn: int32 [16384, 27], P(('grp', 'sub')), may hold values from 0 to 16383, as said below
Outputs:
- solution: float32 [96, 131072], P(None, ('grp', 'sub'))
- residual: float32 [96, 131072], P(None, ('grp', 'sub'))
Inputs may be any that keep to these rules, and one draw needn't show every extreme that they name: `blocks`: entries at positions 6561 and beyond are zero. `owners`: in each device's 128 rows at most 48 name the same column. `conn`: A column's nodes form layers of 128 nodes, node n in layer n // 128. An element in the rows of the device at position s along sub touches three consecutive layers, all within nodes s * 1024 to (s + 1) * 1024 + 2 * 128 - 1 of its column (within the column).
All inputs are finite; a program needn't handle non-finite values.
Results may differ from a plain program's by a relative error of at most 0.0075.
Values may be sent and summed in bfloat16 or wider, within the bound.
A program may use at most 192 MiB of HBM per device.

v0:
```python
import jax
import jax.numpy as jnp
from jax import lax
from jax.sharding import PartitionSpec as P

STEPS = 2
epsilon = 1e-06


def passed_along(block, axis, distance):
    devices = range(lax.axis_size(axis))
    route = [(i - distance, i) for i in devices if i - distance in devices]
    return lax.ppermute(block, axis, route)


def place_blocks(blocks, owners, conn, groups, capacity):
    owner_group = owners[:, 0]
    onehot = (owner_group[:, None] == jnp.arange(groups, dtype=jnp.int32)[None, :]).astype(
        jnp.int32
    )
    before = jnp.cumsum(onehot, axis=0) - onehot
    position = jnp.sum(before * onehot, axis=1)
    target = owner_group * capacity + position
    send_blocks = (
        jnp.zeros((groups * capacity, blocks.shape[1]), blocks.dtype).at[target].set(blocks)
    )
    send_links = jnp.zeros((groups * capacity, conn.shape[1]), jnp.int32).at[target].set(conn)
    return (send_blocks.reshape(groups, capacity, -1), send_links.reshape(groups, capacity, -1))


def window_product(matrix_groups, link_groups, field):
    rows = field.shape[0]
    window = field.shape[1]
    places = jnp.arange(window, dtype=jnp.int32)

    def one_group(acc, pair):
        matrix, links = pair
        slot_count = matrix.shape[0]
        selector = (links[:, None] == places[None, :]).astype(jnp.bfloat16)
        picked = jnp.einsum(
            "rw,lw->rl", field, selector, preferred_element_type=jnp.float32
        ).astype(jnp.bfloat16)
        picked = picked.reshape(3, rows // 3, slot_count, 27)
        result = jnp.einsum("spcqd,cosp->dosq", matrix, picked, preferred_element_type=jnp.float32)
        result = result.reshape(rows, slot_count * 27)
        high_part = result.astype(jnp.bfloat16)
        low_part = (result - high_part.astype(jnp.float32)).astype(jnp.bfloat16)
        acc = acc + jnp.dot(high_part, selector, preferred_element_type=jnp.float32)
        acc = acc + jnp.dot(low_part, selector, preferred_element_type=jnp.float32)
        return (acc, None)

    start = jnp.zeros((rows, window), jnp.float32)
    acc, unused = lax.scan(one_group, start, (matrix_groups, link_groups))
    return acc


def column_sums(first, second):
    return jnp.sum((first * second).reshape(3, -1, first.shape[1]), axis=(0, 2))


def update(solution, residual, image, along, energy):
    alpha = along / (energy + epsilon)
    scale_rows = jnp.tile(alpha, 3)[:, None]
    return (solution + scale_rows * residual, residual - scale_rows * image)


def shards(rhs, blocks, owners, conn):
    groups = lax.axis_size("grp")
    held = blocks.shape[0]
    capacity = max(2, 3 * held // 8)
    send_blocks, send_links = place_blocks(blocks, owners, conn, groups, capacity)
    got_blocks, got_links = (
        lax.all_to_all(send_blocks, "grp", split_axis=0, concat_axis=0, tiled=True),
        lax.all_to_all(send_links, "grp", split_axis=0, concat_axis=0, tiled=True),
    )
    matrix_groups = got_blocks[:, :, :6561].reshape(groups, capacity, 27, 3, 27, 3)
    residual = rhs
    solution = jnp.zeros(rhs.shape, jnp.float32)
    own_count = rhs.shape[1]
    band_width = 2 * held
    local_links = jnp.clip(
        got_links - lax.axis_index("sub") * own_count, 0, own_count + band_width - 1
    ).astype(jnp.int32)
    link_groups = local_links.reshape(groups, capacity * 27)
    for step in range(STEPS):
        rounded = residual.astype(jnp.bfloat16)
        upper = passed_along(rounded[:, :band_width], "sub", -1)
        field = jnp.concatenate([rounded, upper], axis=1)
        partial_sum = window_product(matrix_groups, link_groups, field)
        incoming = passed_along(partial_sum[:, own_count:], "sub", 1)
        image = partial_sum[:, :own_count] + jnp.pad(
            incoming, ((0, 0), (0, own_count - band_width))
        )
        along, energy = lax.psum(
            (column_sums(residual, image), column_sums(image, image)), ("grp", "sub")
        )
        solution, residual = update(solution, residual, image, along, energy)
    return (solution, residual)


def solution(mesh):
    return jax.shard_map(
        shards,
        mesh=mesh,
        in_specs=(
            P(None, ("grp", "sub")),
            P(("grp", "sub"), None),
            P(("grp", "sub"), None),
            P(("grp", "sub"), None),
        ),
        out_specs=(P(None, ("grp", "sub")), P(None, ("grp", "sub"))),
        check_vma=False,
    )
```

profile of v0, /device:TPU:1, one launch (start us, length us, event | category | flops | bytes accessed | tf_op | source)
XLA Modules:
  0.0 515.8 jit_solution(13757841406392980905)
XLA Ops:
  5.7 6.8 %all-to-all-start = ((s32[8,1,1296]{2,1,0:T(1,128)}), s32[8,1,1296]{2,1,0:T(1,128)S(1)}, u32[]{:S(2)}, u32[]{:S(2)}) async-start(s32[8,1,1296]{2,1,0:T(1,128)} %reshape.81), calls=%async_computation | async-start | bytes 90112 | tf_op jit(solution)/shard_map/all_to_all | solution.py:74
  12.5 6.9 %scatter_custom_fusion.1 = bf16[384,6656]{1,0:T(8,128)(2,1)} fusion(s32[128]{0:T(128)S(1)} %fusion.50, bf16[128,6656]{1,0:T(8,128)(2,1)} %param.9, bf16[]{:T(256)} %constant.23.clone.1), kind=kCustom, calls=%fused_computation.46 | custom fusion | bytes 5112320 | tf_op jit(solution)/shard_map/scatter | solution.py:25
  19.5 4.9 all-to-all-start.1
  29.8 53.3 %all-to-all-done.1 = bf16[8,48,6656]{2,1,0:T(8,128)(2,1)} async-done(((bf16[8,48,6656]{2,1,0:T(8,128)(2,1)}), bf16[8,48,6656]{2,1,0:T(8,128)(2,1)}, u32[]{:S(2)}, u32[]{:S(2)}) %all-to-all-start.1) | async-done | bytes 5111840 | tf_op jit(solution)/shard_map/all_to_all | solution.py:73
  83.1 14.8 %copy.45 = bf16[8,48,6561]{1,0,2:T(8,128)(2,1)} copy(bf16[8,48,6561]{2,1,0:T(8,128)(2,1)} %bitcast.44) | data formatting | bytes 10077696
  97.9 35.7 %copy.35 = bf16[8,48,27,3,27,3]{4,2,3,5,1,0:T(8,128)(2,1)} copy(bf16[8,48,27,3,27,3]{1,0,5,4,3,2:T(8,128)(2,1)} %bitcast.67) | data formatting | bytes 10077696
  133.6 112.3 %while.22 = (s32[]{:T(128)}, f32[96,1280]{1,0:T(8,128)}, s32[8,1296]{1,0:T(8,128)}, bf16[96,1280]{1,0:T(8,128)(2,1)S(1)}, bf16[8,48,27,3,27,3]{4,2,3,5,1,0:T(8,128)(2,1)}, /*index=5*/s32[]{:T(128)}, s32[]{:T(128)}) while((s32[]{:T(128)}, f32[96,1280]{1,0:T(8,128)}, s32[8,1296]{1,0:T(8,128)}, bf16[96,1280]{1,0:T(8,128)(2,1)S(1)}, ...), condition=%wide.region_5.6_spmd.clone, body=%wide.region_4.5_spmd.clone.sunk | while | flops 981762048 | bytes 10256283 | solution.py:53
  137.7 2.8 fusion.75
  150.8 2.8 fusion.75
  156.0 2.6 fusion.76
  165.0 2.8 fusion.75
  170.2 2.6 fusion.76
  179.1 2.8 fusion.75
  184.3 2.6 fusion.76
  193.3 2.8 fusion.75
  198.5 2.6 fusion.76
  207.5 2.8 fusion.75
  221.6 2.8 fusion.75
  235.8 2.8 fusion.75
  246.8 3.2 collective-permute-start.1
  253.0 66.9 %all-reduce.3 = (f32[32]{0:T(128)S(1)}, f32[32]{0:T(128)S(1)}) all-reduce(f32[32]{0:T(128)S(1)} %reduce_sum.62, f32[32]{0:T(128)S(1)} %reduce_sum.82), channel_id=1, replica_groups=mesh['grp'=8,'sub'=16] {'grp','sub'}, use_global_device_ids=true, to_apply=%region_8.9 | all-reduce | flops 64 | bytes 512 | tf_op jit(solution)/shard_map/psum | solution.py:94
  323.4 3.3 collective-permute-done.2
  326.7 112.3 %while.23 = (s32[]{:T(128)}, f32[96,1280]{1,0:T(8,128)}, s32[8,1296]{1,0:T(8,128)}, bf16[96,1280]{1,0:T(8,128)(2,1)S(1)}, bf16[8,48,27,3,27,3]{4,2,3,5,1,0:T(8,128)(2,1)}, /*index=5*/s32[]{:T(128)}, s32[]{:T(128)}) while((s32[]{:T(128)}, f32[96,1280]{1,0:T(8,128)}, s32[8,1296]{1,0:T(8,128)}, bf16[96,1280]{1,0:T(8,128)(2,1)S(1)}, ...), condition=%wide.region_13.14_spmd.clone, body=%wide.region_12.13_spmd.clone.sunk | while | flops 981762048 | bytes 10256283 | solution.py:53
  330.8 2.8 fusion.83
  343.9 2.8 fusion.83
  358.1 2.8 fusion.83
  372.3 2.8 fusion.83
  386.4 2.8 fusion.83
  400.6 2.8 fusion.83
  414.7 2.8 fusion.83
  428.9 2.8 fusion.83
  445.6 68.0 %all-reduce.2 = (f32[32]{0:T(128)S(1)}, f32[32]{0:T(128)S(1)}) all-reduce(f32[32]{0:T(128)S(1)} %reduce_sum.85, f32[32]{0:T(128)S(1)} %reduce_sum.88), channel_id=1, replica_groups=mesh['grp'=8,'sub'=16] {'grp','sub'}, use_global_device_ids=true, to_apply=%region_16.17 | all-reduce | flops 64 | bytes 512 | tf_op jit(solution)/shard_map/psum | solution.py:94
  (158 shorter events, 195.2 us)
Async XLA Ops:
  5.7 13.8 %all-to-all-start = ((s32[8,1,1296]{2,1,0:T(1,128)}), s32[8,1,1296]{2,1,0:T(1,128)S(1)}, u32[]{:S(2)}, u32[]{:S(2)}) async-start(s32[8,1,1296]{2,1,0:T(1,128)} %reshape.81), calls=%async_computation | async-start | bytes 90112 | tf_op jit(solution)/shard_map/all_to_all | solution.py:74
  19.5 4.9 copy-start
  19.5 63.7 %all-to-all-start.1 = ((bf16[8,48,6656]{2,1,0:T(8,128)(2,1)}), bf16[8,48,6656]{2,1,0:T(8,128)(2,1)}, u32[]{:S(2)}, u32[]{:S(2)}) async-start(bf16[8,48,6656]{2,1,0:T(8,128)(2,1)} %bitcast.68), calls=%async_computation.1 | async-start | bytes 10223616 | tf_op jit(solution)/shard_map/all_to_all | solution.py:73
  24.4 5.4 %collective-permute-start = (bf16[96,256]{1,0:T(8,128)(2,1)S(1)}, bf16[96,256]{1,0:T(8,128)(2,1)S(1)}, u32[]{:S(2)}, u32[]{:S(2)}) collective-permute-start(bf16[96,256]{1,0:T(8,128)(2,1)S(1)} %slice.28), channel_id=1, source_target_pairs={{1,0},{2,1},{3,2},{4,3},{5,4},{6,5},{7,6},{8,7},{9,8},{10,9},{11,1... | collective-permute-start | bytes 147464 | tf_op jit(solution)/shard_map/ppermute | solution.py:13
  246.8 4.8 collective-permute-start.1
  321.9 4.8 collective-permute-start.2
  439.9 4.1 collective-permute-start.3
where the time goes:
time: 520 us; the launch traced here: 516 us
  matrix products  147 us (28%)
  local copies, waits for them, and re-layouts  141 us (27%)
  blocking collectives  135 us (26%)
  waiting for transfers between devices  61.3 us (12%)
  starting transfers between devices  20.5 us (4%)
  other arithmetic  9.82 us (2%)
    psum x2, blocking collectives, shards(): lax.psum((column_sums(residual, image), column_sums(image, image)), ('grp...  135 us
    all_to_all x1, waiting for transfers between devices, shards(): lax.all_to_all(send_blocks, 'grp', split_axis=0, concat_axis=0, tiled=True)  53.3 us
    unnamed x7, local copies, waits for them, and re-layouts  52.2 us
    dot_general x16, matrix products, one_group(): jnp.einsum('spcqd,cosp->dosq', matrix, picked, preferred_element_type=jnp...  44.9 us
    dot_general x16, matrix products, one_group(): acc = acc + jnp.dot(high_part, selector, preferred_element_type=jnp.float32)  39.2 us
    dot_general x16, matrix products, one_group(): acc = acc + jnp.dot(low_part, selector, preferred_element_type=jnp.float32)  37.2 us
    reshape x16, local copies, waits for them, and re-layouts, one_group(): picked = picked.reshape(3, rows // 3, slot_count, 27)  26.4 us
    dot_general x16, matrix products, one_group(): jnp.einsum('rw,lw->rl', field, selector, preferred_element_type=jnp.float32)  25.1 us
  transfers between devices with their start and end apart: 6, of which 5 were waited for; matrix products, arithmetic and copies ran while one was open for 2% of the time, Pallas kernels for 0%

commit v1 on v0

--- a/solution.py
+++ b/solution.py
@@ -92,7 +92,7 @@
             incoming, ((0, 0), (0, own_count - band_width))
         )
         along, energy = lax.psum(
-            (column_sums(residual, image), column_sums(image, image)), ("grp", "sub")
+            lax.psum((column_sums(residual, image), column_sums(image, image)), "grp"), "sub"
         )
         solution, residual = update(solution, residual, image, along, energy)
     return (solution, residual)

time: 520 us -> 490 us (0.942)
  the two profiles are of different devices: /device:TPU:1 before, /device:TPU:0 now
where the time goes in v1:
time: 490 us; the launch traced here: 486 us
  matrix products  147 us (30%)
  local copies, waits for them, and re-layouts  141 us (29%)
  blocking collectives  104 us (21%)
  waiting for transfers between devices  64.5 us (13%)
  starting transfers between devices  18.4 us (4%)
  other arithmetic  9.83 us (2%)
    psum x2, blocking collectives, shards(): lax.psum(lax.psum((column_sums(residual, image), column_sums(image, image...  79.3 us
    all_to_all x1, waiting for transfers between devices, shards(): lax.all_to_all(send_blocks, 'grp', split_axis=0, concat_axis=0, tiled=True)  53.5 us
    unnamed x7, local copies, waits for them, and re-layouts  52.2 us
    dot_general x16, matrix products, one_group(): jnp.einsum('spcqd,cosp->dosq', matrix, picked, preferred_element_type=jnp...  44.9 us
    dot_general x16, matrix products, one_group(): acc = acc + jnp.dot(high_part, selector, preferred_element_type=jnp.float32)  39.2 us
    dot_general x16, matrix products, one_group(): acc = acc + jnp.dot(low_part, selector, preferred_element_type=jnp.float32)  37.2 us
    reshape x16, local copies, waits for them, and re-layouts, one_group(): picked = picked.reshape(3, rows // 3, slot_count, 27)  26.4 us
    dot_general x16, matrix products, one_group(): jnp.einsum('rw,lw->rl', field, selector, preferred_element_type=jnp.float32)  25.1 us
  transfers between devices with their start and end apart: 6, of which 5 were waited for; matrix products, arithmetic and copies ran while one was open for 2% of the time, Pallas kernels for 0%

profile of v1, /device:TPU:0, one launch (start us, length us, event | category | flops | bytes accessed | tf_op | source)
XLA Modules:
  0.0 486.1 jit_solution(8484267942732070464)
XLA Ops:
  5.7 5.4 %all-to-all-start = ((s32[8,1,1296]{2,1,0:T(1,128)}), s32[8,1,1296]{2,1,0:T(1,128)S(1)}, u32[]{:S(2)}, u32[]{:S(2)}) async-start(s32[8,1,1296]{2,1,0:T(1,128)} %reshape.81), calls=%async_computation | async-start | bytes 90112 | tf_op jit(solution)/shard_map/all_to_all | solution.py:74
  11.1 6.9 %scatter_custom_fusion.1 = bf16[384,6656]{1,0:T(8,128)(2,1)} fusion(s32[128]{0:T(128)S(1)} %fusion.50, bf16[128,6656]{1,0:T(8,128)(2,1)} %param.9, bf16[]{:T(256)} %constant.23.clone.1), kind=kCustom, calls=%fused_computation.46 | custom fusion | bytes 5112320 | tf_op jit(solution)/shard_map/scatter | solution.py:25
  18.1 4.9 %all-to-all-start.1 = ((bf16[8,48,6656]{2,1,0:T(8,128)(2,1)}), bf16[8,48,6656]{2,1,0:T(8,128)(2,1)}, u32[]{:S(2)}, u32[]{:S(2)}) async-start(bf16[8,48,6656]{2,1,0:T(8,128)(2,1)} %bitcast.68), calls=%async_computation.1 | async-start | bytes 10223616 | tf_op jit(solution)/shard_map/all_to_all | solution.py:73
  29.1 53.5 %all-to-all-done.1 = bf16[8,48,6656]{2,1,0:T(8,128)(2,1)} async-done(((bf16[8,48,6656]{2,1,0:T(8,128)(2,1)}), bf16[8,48,6656]{2,1,0:T(8,128)(2,1)}, u32[]{:S(2)}, u32[]{:S(2)}) %all-to-all-start.1) | async-done | bytes 5111840 | tf_op jit(solution)/shard_map/all_to_all | solution.py:73
  82.6 14.8 %copy.45 = bf16[8,48,6561]{1,0,2:T(8,128)(2,1)} copy(bf16[8,48,6561]{2,1,0:T(8,128)(2,1)} %bitcast.44) | data formatting | bytes 10077696
  97.4 35.7 %copy.35 = bf16[8,48,27,3,27,3]{4,2,3,5,1,0:T(8,128)(2,1)} copy(bf16[8,48,27,3,27,3]{1,0,5,4,3,2:T(8,128)(2,1)} %bitcast.67) | data formatting | bytes 10077696
  133.1 112.3 %while.22 = (s32[]{:T(128)}, f32[96,1280]{1,0:T(8,128)}, s32[8,1296]{1,0:T(8,128)}, bf16[96,1280]{1,0:T(8,128)(2,1)S(1)}, bf16[8,48,27,3,27,3]{4,2,3,5,1,0:T(8,128)(2,1)}, /*index=5*/s32[]{:T(128)}, s32[]{:T(128)}) while((s32[]{:T(128)}, f32[96,1280]{1,0:T(8,128)}, s32[8,1296]{1,0:T(8,128)}, bf16[96,1280]{1,0:T(8,128)(2,1)S(1)}, ...), condition=%wide.region_5.6_spmd.clone, body=%wide.region_4.5_spmd.clone.sunk | while | flops 981762048 | bytes 10256283 | solution.py:53
  137.1 2.8 fusion.75
  150.3 2.8 fusion.75
  155.5 2.6 fusion.76
  164.4 2.8 fusion.75
  169.6 2.6 fusion.76
  178.6 2.8 fusion.75
  192.7 2.8 fusion.75
  206.9 2.8 fusion.75
  221.1 2.8 fusion.75
  235.2 2.8 fusion.75
  246.3 3.5 collective-permute-start.1
  253.3 12.4 %all-reduce.5 = (f32[32]{0:T(128)S(1)}, f32[32]{0:T(128)S(1)}) all-reduce(f32[32]{0:T(128)S(1)} %reduce_sum.62, f32[32]{0:T(128)S(1)} %reduce_sum.82), channel_id=1, replica_groups=mesh['grp'=8,'sub'=16] {'grp'}, use_global_device_ids=true, to_apply=%region_8.9 | all-reduce | flops 64 | bytes 512 | tf_op jit(solution)/shard_map/psum | solution.py:95
  265.7 41.5 %all-reduce.3 = (f32[32]{0:T(128)S(1)}, f32[32]{0:T(128)S(1)}) all-reduce(f32[32]{0:T(128)S(1)} %get-tuple-element.168, f32[32]{0:T(128)S(1)} %get-tuple-element.169), channel_id=1, replica_groups=mesh['grp'=8,'sub'=16] {'sub'}, use_global_device_ids=true, to_apply=%region_9.10 | all-reduce | flops 64 | bytes 512 | tf_op jit(solution)/shard_map/psum | solution.py:94
  310.7 4.5 collective-permute-done.2
  315.2 112.3 %while.23 = (s32[]{:T(128)}, f32[96,1280]{1,0:T(8,128)}, s32[8,1296]{1,0:T(8,128)}, bf16[96,1280]{1,0:T(8,128)(2,1)S(1)}, bf16[8,48,27,3,27,3]{4,2,3,5,1,0:T(8,128)(2,1)}, /*index=5*/s32[]{:T(128)}, s32[]{:T(128)}) while((s32[]{:T(128)}, f32[96,1280]{1,0:T(8,128)}, s32[8,1296]{1,0:T(8,128)}, bf16[96,1280]{1,0:T(8,128)(2,1)S(1)}, ...), condition=%wide.region_15.16_spmd.clone, body=%wide.region_14.15_spmd.clone.sunk | while | flops 981762048 | bytes 10256283 | solution.py:53
  319.2 2.8 fusion.83
  332.4 2.8 fusion.83
  346.5 2.8 fusion.83
  360.7 2.8 fusion.83
  374.8 2.8 fusion.83
  389.0 2.8 fusion.83
  403.2 2.8 fusion.83
  417.3 2.8 fusion.83
  433.6 12.4 %all-reduce.4 = (f32[32]{0:T(128)S(1)}, f32[32]{0:T(128)S(1)}) all-reduce(f32[32]{0:T(128)S(1)} %reduce_sum.85, f32[32]{0:T(128)S(1)} %reduce_sum.88), channel_id=1, replica_groups=mesh['grp'=8,'sub'=16] {'grp'}, use_global_device_ids=true, to_apply=%region_18.19 | all-reduce | flops 64 | bytes 512 | tf_op jit(solution)/shard_map/psum | solution.py:95
  446.1 37.8 %all-reduce.2 = (f32[32]{0:T(128)S(1)}, f32[32]{0:T(128)S(1)}) all-reduce(f32[32]{0:T(128)S(1)} %get-tuple-element.166, f32[32]{0:T(128)S(1)} %get-tuple-element.167), channel_id=1, replica_groups=mesh['grp'=8,'sub'=16] {'sub'}, use_global_device_ids=true, to_apply=%region_19.20 | all-reduce | flops 64 | bytes 512 | tf_op jit(solution)/shard_map/psum | solution.py:94
  (160 shorter events, 201.3 us)
Async XLA Ops:
  5.7 12.3 %all-to-all-start = ((s32[8,1,1296]{2,1,0:T(1,128)}), s32[8,1,1296]{2,1,0:T(1,128)S(1)}, u32[]{:S(2)}, u32[]{:S(2)}) async-start(s32[8,1,1296]{2,1,0:T(1,128)} %reshape.81), calls=%async_computation | async-start | bytes 90112 | tf_op jit(solution)/shard_map/all_to_all | solution.py:74
  18.0 4.9 %copy-start = (f32[96,1024]{1,0:T(8,128)S(1)}, f32[96,1024]{1,0:T(8,128)}, u32[]{:S(2)}) copy-start(f32[96,1024]{1,0:T(8,128)} %param.8) | copy-start | bytes 1179652
  18.1 64.5 %all-to-all-start.1 = ((bf16[8,48,6656]{2,1,0:T(8,128)(2,1)}), bf16[8,48,6656]{2,1,0:T(8,128)(2,1)}, u32[]{:S(2)}, u32[]{:S(2)}) async-start(bf16[8,48,6656]{2,1,0:T(8,128)(2,1)} %bitcast.68), calls=%async_computation.1 | async-start | bytes 10223616 | tf_op jit(solution)/shard_map/all_to_all | solution.py:73
  23.0 6.0 %collective-permute-start = (bf16[96,256]{1,0:T(8,128)(2,1)S(1)}, bf16[96,256]{1,0:T(8,128)(2,1)S(1)}, u32[]{:S(2)}, u32[]{:S(2)}) collective-permute-start(bf16[96,256]{1,0:T(8,128)(2,1)S(1)} %slice.28), channel_id=1, source_target_pairs={{1,0},{2,1},{3,2},{4,3},{5,4},{6,5},{7,6},{8,7},{9,8},{10,9},{11,1... | collective-permute-start | bytes 147464 | tf_op jit(solution)/shard_map/ppermute | solution.py:13
  246.3 5.7 %collective-permute-start.1 = (f32[96,256]{1,0:T(8,128)S(1)}, f32[96,256]{1,0:T(8,128)S(1)}, u32[]{:S(2)}, u32[]{:S(2)}) collective-permute-start(f32[96,256]{1,0:T(8,128)S(1)} %slice.24), channel_id=1, source_target_pairs={{0,1},{1,2},{2,3},{3,4},{4,5},{5,6},{6,7},{7,8},{8,9},{9,10},{10,1... | collective-permute-start | bytes 294920 | tf_op jit(solution)/shard_map/ppermute | solution.py:13
  309.2 6.0 %collective-permute-start.2 = (bf16[96,256]{1,0:T(8,128)(2,1)S(1)}, bf16[96,256]{1,0:T(8,128)(2,1)S(1)}, u32[]{:S(2)}, u32[]{:S(2)}) collective-permute-start(bf16[96,256]{1,0:T(8,128)(2,1)S(1)} %slice.30), channel_id=1, source_target_pairs={{1,0},{2,1},{3,2},{4,3},{5,4},{6,5},{7,6},{8,7},{9,8},{10,9},{11,1... | collective-permute-start | bytes 147464 | tf_op jit(solution)/shard_map/ppermute | solution.py:13
  428.4 3.8 collective-permute-start.3
